TPU v7x, 32 devices: a whole 2x2x4 slice. The times are simulated.
32 devices in a mesh: dp: 8 (over y, x, core), ctx: 4 (over z).
Axes of the slice: x: 2, y: 2, z: 4, core: 2. Of those that a mesh axis runs over, the one named last changes fastest.
Arguments:
- inputs: bfloat16 [8, 512, 2048], P('dp', 'ctx'), may hold values from -6 to 6
- segment: int32 [8, 512], P('dp', 'ctx'), may hold values from 0 to 3, as said below
- w_qkv: bfloat16 [2048, 6144], P(('dp', 'ctx')), may hold values from -0.125 to 0.125
- w_out: bfloat16 [2048, 2048], P(('dp', 'ctx')), may hold values from -0.125 to 0.125
- w_gate: bfloat16 [2048, 8192], P('dp', 'ctx'), may hold values from -0.125 to 0.125
- w_up: bfloat16 [2048, 8192], P('dp', 'ctx'), may hold values from -0.125 to 0.125
- w_down_t: bfloat16 [2048, 8192], P('dp', 'ctx'), may hold values from -0.0625 to 0.0625
- gains: float32 [4, 2048], replicated, may hold values from 0.25 to 1.75
- cotangent: bfloat16 [8, 512, 2048], P('dp', 'ctx'), may hold values from -6 to 6
Outputs:
- output: bfloat16 [8, 512, 2048], P('dp', 'ctx')
- input_grad: float32 [8, 512, 2048], P('dp', 'ctx')
- grad_qkv: float32 [2048, 6144], P(('dp', 'ctx'))
- grad_out: float32 [2048, 2048], P(('dp', 'ctx'))
- grad_gate: float32 [2048, 8192], P('dp', 'ctx')
- grad_up: float32 [2048, 8192], P('dp', 'ctx')
- grad_down_t: float32 [2048, 8192], P('dp', 'ctx')
- grad_gains: float32 [4, 2048], replicated
Inputs may be any that keep to these rules, and one draw needn't show every extreme that they name: `segment`: in every sequence ids 1, 2 and 3 mark three documents in this order, each of one position or more, and 0 marks padding, one position or more at the sequence's end.
All inputs are finite; a program needn't handle non-finite values.
Results may differ from a plain program's by a relative error of at most 0.015.
Values may be sent and summed in bfloat16 or wider, within the bound.
A program may use at most 704 MiB of HBM per device.

v0:
```python
import jax
import jax.numpy as jnp
from jax import lax
from jax.sharding import Mesh
from jax.sharding import PartitionSpec as P

HEAD_DIM = 128
EPS = 1e-06
ROPE_BASE = 500000.0
F32 = jnp.float32
BF16 = jnp.bfloat16
GROUP = ("core", "ctx")
ALL = ("chip", "core", "ctx")


def rope_tables(positions):
    half = HEAD_DIM // 2
    frequency = ROPE_BASE ** (-(jnp.arange(half, dtype=F32) * 2.0 / HEAD_DIM))
    angles = positions[:, None] * frequency[None, :]
    cosine = jnp.cos(angles)
    sine = jnp.sin(angles)
    return (jnp.concatenate([cosine, cosine], 1), jnp.concatenate([sine, sine], 1))


def rotate(values, cosine, sine):
    half = HEAD_DIM // 2
    turned = jnp.concatenate([-values[..., half:], values[..., :half]], -1)
    return values * cosine + turned * sine


def rotate_back(values, cosine, sine):
    half = HEAD_DIM // 2
    scaled = values * sine
    turned = jnp.concatenate([scaled[..., half:], -scaled[..., :half]], -1)
    return values * cosine + turned


def dot(left, right):
    return jnp.dot(left, right, preferred_element_type=F32)


def dot_rows(left, right):
    return lax.dot_general(left, right, (((1,), (1,)), ((), ())), preferred_element_type=F32)


def dot_first(left, right):
    return lax.dot_general(left, right, (((0,), (0,)), ((), ())), preferred_element_type=F32)


def gather(values, axes):
    return lax.all_gather(values, axes, axis=0, tiled=True)


def scatter_sum(values, axes):
    return lax.psum_scatter(values, axes, scatter_dimension=0, tiled=True)


def norm_factor(values):
    return lax.rsqrt(jnp.mean(values * values, axis=-1, keepdims=True) + EPS)


def norm_back(values, factor, gain, grad):
    normed = values * factor
    scaled = gain * grad
    back = factor * (scaled - normed * jnp.mean(scaled * normed, axis=-1, keepdims=True))
    return (back, jnp.sum(grad * normed, axis=0))


def per_device(inputs, segment, w_qkv, w_out, w_gate, w_up, w_down_t, gains, cotangent):
    rows, width = inputs.shape[1:]
    cores = lax.axis_size("core")
    spans = lax.axis_size("ctx")
    members = cores * spans
    length = rows * spans
    total_rows = cores * length
    part = width // members
    heads = part // HEAD_DIM
    member = lax.axis_index(GROUP)
    tokens = inputs[0]
    qkv_rows = w_qkv.shape[0]
    qkv_cut = w_qkv.reshape(qkv_rows, 3, members, part).transpose(2, 0, 1, 3)
    qkv_cut = qkv_cut.reshape(members, qkv_rows, 3 * part)
    qkv_cut = lax.all_to_all(qkv_cut, GROUP, 0, 0, tiled=True)
    qkv_w = gather(qkv_cut.reshape(members * qkv_rows, 3 * part), "chip")
    tokens_all = gather(tokens, GROUP)
    out_full = gather(w_out, ALL)
    out_w = lax.dynamic_slice_in_dim(out_full, member * part, part, 0)
    hidden = w_gate.shape[1] // cores
    gate_up = jnp.concatenate(
        [w_gate.reshape(-1, cores, 1, hidden), w_up.reshape(-1, cores, 1, hidden)], 2
    ).reshape(-1, cores * 2 * hidden)
    gate_up = lax.all_to_all(gate_up, "core", 1, 0, tiled=True)
    gate_up_w = gather(gate_up, "chip")
    down_w = gather(lax.all_to_all(w_down_t, "core", 1, 0, tiled=True), "chip")
    mixed = dot(tokens_all, qkv_w)
    query_raw = mixed[:, :part]
    key_raw = mixed[:, part : 2 * part]
    value_low = mixed[:, 2 * part :].astype(BF16)
    squares = jnp.stack([jnp.sum(query_raw * query_raw, 1), jnp.sum(key_raw * key_raw, 1)])
    squares = lax.psum(squares, GROUP)
    factors = lax.rsqrt(squares / width + EPS)
    gain_q = lax.dynamic_slice_in_dim(gains[0], member * part, part)
    gain_k = lax.dynamic_slice_in_dim(gains[1], member * part, part)
    places = jnp.arange(length, dtype=jnp.int32)
    cosine, sine = rope_tables(places.astype(F32))
    cosine, sine = (cosine[None, :, None, :], sine[None, :, None, :])
    shape = (cores, length, heads, HEAD_DIM)
    query_factor, key_factor = (factors[0][:, None], factors[1][:, None])
    query_low = rotate((query_raw * query_factor * gain_q).reshape(shape), cosine, sine).astype(
        BF16
    )
    key_low = rotate((key_raw * key_factor * gain_k).reshape(shape), cosine, sine).astype(BF16)
    value_low = value_low.reshape(shape)
    ids = gather(segment[0], GROUP).reshape(cores, length)
    allowed = (
        (ids[:, :, None] == ids[:, None, :])
        & (places[None, None, :] <= places[None, :, None])
        & ((ids[:, None, :] != 0) | (places[None, None, :] == places[None, :, None]))
    )[:, None]
    scale = HEAD_DIM ** (-0.5)
    scores = jnp.einsum("bqhd,bkhd->bhqk", query_low, key_low, preferred_element_type=F32) * scale
    masked = jnp.where(allowed, scores, -1e30)
    row_max = jnp.max(masked, axis=-1, keepdims=True)
    weights = jnp.where(allowed, jnp.exp(masked - row_max), 0.0)
    shares = weights / jnp.sum(weights, axis=-1, keepdims=True)
    shares_low = shares.astype(BF16)
    attended = jnp.einsum("bhqk,bkhd->bqhd", shares_low, value_low, preferred_element_type=F32)
    attended_low = attended.reshape(total_rows, part).astype(BF16)
    projected = scatter_sum(dot(attended_low, out_w).astype(BF16), GROUP).astype(F32)
    tokens_wide = tokens.astype(F32)
    proj_factor = norm_factor(projected)
    residual = tokens_wide + projected * proj_factor * gains[2]
    residual_all = gather(residual.astype(BF16), GROUP)
    gate_up_out = dot(residual_all, gate_up_w)
    gate, up_part = (gate_up_out[:, :hidden], gate_up_out[:, hidden:])
    sigmoid = 1.0 / (1.0 + jnp.exp(-gate))
    activated = (gate * sigmoid * up_part).astype(BF16)
    feed = scatter_sum(dot_rows(activated, down_w).astype(BF16), GROUP).astype(F32)
    feed_factor = norm_factor(feed)
    output = (residual + feed * feed_factor * gains[3]).astype(BF16)
    upstream = cotangent[0].astype(F32)
    feed_grad, gain_feed = norm_back(feed, feed_factor, gains[3], upstream)
    feed_grad_all = gather(feed_grad.astype(BF16), GROUP)
    act_grad = dot(feed_grad_all, down_w)
    gate_grad = act_grad * up_part * sigmoid * (1.0 + gate * (1.0 - sigmoid))
    up_grad = act_grad * (gate * sigmoid)
    gate_up_grad = jnp.concatenate([gate_grad.astype(BF16), up_grad.astype(BF16)], 1)
    back_feed = scatter_sum(dot_rows(gate_up_grad, gate_up_w).astype(BF16), GROUP).astype(F32)
    residual_grad = upstream + back_feed
    grad_gate_up = scatter_sum(dot_first(residual_all, gate_up_grad).astype(BF16), "chip")
    grad_gate_up = lax.all_to_all(grad_gate_up, "core", 0, 1, tiled=True)
    grad_gate_up = grad_gate_up.reshape(-1, cores, 2, hidden).astype(F32)
    grad_gate = grad_gate_up[:, :, 0].reshape(-1, cores * hidden)
    grad_up = grad_gate_up[:, :, 1].reshape(-1, cores * hidden)
    grad_down = scatter_sum(dot_first(feed_grad_all, activated).astype(BF16), "chip")
    grad_down = lax.all_to_all(grad_down, "core", 0, 1, tiled=True).astype(F32)
    projected_grad, gain_attn = norm_back(projected, proj_factor, gains[2], residual_grad)
    projected_all = gather(projected_grad.astype(BF16), GROUP)
    attended_grad = dot_rows(projected_all, out_w).astype(BF16).reshape(shape)
    share_grad = jnp.einsum("bqhd,bkhd->bhqk", attended_grad, value_low, preferred_element_type=F32)
    inner = jnp.sum(shares * share_grad, axis=-1, keepdims=True)
    score_grad = (shares * (share_grad - inner)).astype(BF16)
    query_grad = jnp.einsum("bhqk,bkhd->bqhd", score_grad, key_low, preferred_element_type=F32)
    key_grad = jnp.einsum("bhqk,bqhd->bkhd", score_grad, query_low, preferred_element_type=F32)
    value_grad = jnp.einsum(
        "bhqk,bqhd->bkhd", shares_low, attended_grad, preferred_element_type=F32
    )
    query_turn = rotate_back(query_grad * scale, cosine, sine).reshape(total_rows, part)
    key_turn = rotate_back(key_grad * scale, cosine, sine).reshape(total_rows, part)
    query_norm, key_norm = (query_raw * query_factor, key_raw * key_factor)
    sums = jnp.stack(
        [jnp.sum(gain_q * query_turn * query_norm, 1), jnp.sum(gain_k * key_turn * key_norm, 1)]
    )
    means = lax.psum(sums, GROUP) / width
    query_mixed = query_factor * (gain_q * query_turn - query_norm * means[0][:, None])
    key_mixed = key_factor * (gain_k * key_turn - key_norm * means[1][:, None])
    gain_query = jnp.sum(query_turn * query_norm, 0)
    gain_key = jnp.sum(key_turn * key_norm, 0)
    mixed_grad = jnp.concatenate(
        [query_mixed, key_mixed, value_grad.reshape(total_rows, part)], 1
    ).astype(BF16)
    input_part = dot_rows(mixed_grad, qkv_w).astype(BF16)
    input_grad = residual_grad + scatter_sum(input_part, GROUP).astype(F32)
    grad_qkv = scatter_sum(dot_first(tokens_all, mixed_grad).astype(BF16), "chip")
    grad_qkv = grad_qkv.reshape(members, qkv_rows, 3 * part)
    grad_qkv = lax.all_to_all(grad_qkv, GROUP, 0, 0, tiled=True)
    grad_qkv = grad_qkv.reshape(members, qkv_rows, 3, part).transpose(1, 2, 0, 3)
    grad_qkv = grad_qkv.reshape(qkv_rows, 3 * width).astype(F32)
    out_part = dot_first(attended_low, projected_all).astype(BF16)
    out_part = lax.dynamic_update_slice_in_dim(
        jnp.zeros((width, width), BF16), out_part, member * part, 0
    )
    grad_out = scatter_sum(out_part, ALL).astype(F32)
    wide = jnp.zeros((2, width), F32)
    wide = lax.dynamic_update_slice(wide, jnp.stack([gain_query, gain_key]), (0, member * part))
    grad_gains = lax.psum(jnp.concatenate([wide, gain_attn[None], gain_feed[None]]), ALL)
    return (
        output[None],
        input_grad[None],
        grad_qkv,
        grad_out,
        grad_gate,
        grad_up,
        grad_down,
        grad_gains,
    )


def solution(mesh):
    cores = 2
    chips = mesh.shape["dp"] // cores
    split = Mesh(mesh.devices.reshape(chips, cores, mesh.shape["ctx"]), ALL)
    dp = ("chip", "core")
    every = P((*dp, "ctx"), None)
    in_specs = (
        P(dp, "ctx", None),
        P(dp, "ctx"),
        every,
        every,
        P(dp, "ctx"),
        P(dp, "ctx"),
        P(dp, "ctx"),
        P(),
        P(dp, "ctx", None),
    )
    out_specs = (
        P(dp, "ctx", None),
        P(dp, "ctx", None),
        every,
        every,
        P(dp, "ctx"),
        P(dp, "ctx"),
        P(dp, "ctx"),
        P(),
    )
    return jax.shard_map(
        per_device, mesh=split, in_specs=in_specs, out_specs=out_specs, check_vma=False
    )
```

profile of v0, /device:TPU:0, one launch (start us, length us, event | category | flops | bytes accessed | tf_op | source)
XLA Modules:
  0.0 1303.3 jit_solution(13197521999439722919)
XLA Ops:
  9.9 26.9 %all_to_all.74 = bf16[8,64,768]{2,1,0:T(8,128)(2,1)} all-to-all(bf16[8,64,768]{2,1,0:T(8,128)(2,1)S(1)} %reshape.177), channel_id=1, replica_groups=mesh['chip'=4,'core'=2,'ctx'=4] {'core','ctx'}, dimensions={0} | all-to-all | bytes 1572864 | tf_op jit(solution)/shard_map/all_to_all | solution.py:83
  38.3 12.7 all-gather.1
  55.5 23.9 %all-gather.11.cloned.1.call-done = bf16[2048,768]{1,0:T(8,128)(2,1)} async-done(((bf16[512,768]{1,0:T(8,128)(2,1)}), bf16[2048,768]{1,0:T(8,128)(2,1)}) %all-gather.11.cloned.1.call-update) | async-done | bytes 3145744 | tf_op jit(solution)/shard_map/all_gather | solution.py:51
  79.3 48.8 %all-gather.25.cloned.1.call-done = bf16[1,1024,2048]{2,1,0:T(8,128)(2,1)} async-done(((bf16[1,128,2048]{2,1,0:T(8,128)(2,1)}), bf16[1,1024,2048]{2,1,0:T(8,128)(2,1)}) %all-gather.25.cloned.1.call-update) | async-done | bytes 4194320 | tf_op jit(solution)/shard_map/all_gather | solution.py:51
  128.1 6.2 fusion.3
  135.4 15.6 %psum.21 = f32[2,1024]{1,0:T(2,128)S(1)} all-reduce(f32[2,1024]{1,0:T(2,128)S(1)} %pad_maximum_fusion.10), channel_id=1, replica_groups=mesh['chip'=4,'core'=2,'ctx'=4] {'core','ctx'}, use_global_device_ids=true, to_apply=%region_2.0 | all-reduce | flops 2048 | bytes 16384 | tf_op jit(solution)/shard_map/psum | solution.py:100
  152.6 3.1 reshape.181
  155.7 2.6 copy.109
  158.3 3.1 reshape.180
  161.4 2.4 copy.106
  163.8 2.2 reshape.179
  172.5 5.9 fusion.73
  178.4 4.1 fusion.25
  184.5 23.1 %all-gather.13.cloned.1.call-done = bf16[2048,2048]{1,0:T(8,128)(2,1)} async-done(((bf16[64,2048]{1,0:T(8,128)(2,1)}), bf16[2048,2048]{1,0:T(8,128)(2,1)}) %all-gather.13.cloned.1.call-update) | async-done | bytes 8388624 | tf_op jit(solution)/shard_map/all_gather | solution.py:51
  207.6 4.6 convolution_convert_fusion.2
  212.2 2.3 copy.117
  214.5 2.3 copy.118
  218.6 6.3 all_to_all.75
  224.9 3.9 copy.119
  228.9 71.0 %reduce-scatter.9.cloned.1.call-done = bf16[128,2048]{1,0:T(8,128)(2,1)} async-done(((bf16[1024,2048]{1,0:T(8,128)(2,1)}), bf16[128,2048]{1,0:T(8,128)(2,1)}) %reduce-scatter.9.cloned.1.call-update) | async-done | bytes 524304 | tf_op jit(solution)/shard_map/reduce_scatter | solution.py:55
  301.1 2.3 fusion.49
  303.5 2.3 copy.120
  305.7 6.7 all_to_all.76
  312.4 2.4 copy.121
  315.1 74.5 %all-gather.17.cloned.1.call-done = bf16[2048,2048]{1,0:T(8,128)(2,1)} async-done(((bf16[512,2048]{1,0:T(8,128)(2,1)}), bf16[2048,2048]{1,0:T(8,128)(2,1)}) %all-gather.17.cloned.1.call-update) | async-done | bytes 8388624 | tf_op jit(solution)/shard_map/all_gather | solution.py:51
  389.6 49.2 %all-gather.15.cloned.1.call-done = bf16[1024,2048]{1,0:T(8,128)(2,1)} async-done(((bf16[128,2048]{1,0:T(8,128)(2,1)}), bf16[1024,2048]{1,0:T(8,128)(2,1)}) %all-gather.15.cloned.1.call-update) | async-done | bytes 4194320 | tf_op jit(solution)/shard_map/all_gather | solution.py:51
  438.8 12.5 fusion.74
  451.3 3.2 copy-done.7
  454.5 2.7 multiply_convert_fusion.3
  457.2 35.4 %all-gather.19.cloned.1.call-done = bf16[2048,1024]{1,0:T(8,128)(2,1)} async-done(((bf16[512,1024]{1,0:T(8,128)(2,1)}), bf16[2048,1024]{1,0:T(8,128)(2,1)}) %all-gather.19.cloned.1.call-update) | async-done | bytes 4194320 | tf_op jit(solution)/shard_map/all_gather | solution.py:51
  492.7 9.3 convolution_convert_fusion.5
  502.0 89.1 %reduce-scatter.11.cloned.1.call-done = bf16[128,2048]{1,0:T(8,128)(2,1)} async-done(((bf16[1024,2048]{1,0:T(8,128)(2,1)}), bf16[128,2048]{1,0:T(8,128)(2,1)}) %reduce-scatter.11.cloned.1.call-update) | async-done | bytes 524304 | tf_op jit(solution)/shard_map/reduce_scatter | solution.py:55
  594.0 2.4 fusion.28
  596.6 46.8 %all-gather.21.cloned.1.call-done = bf16[1024,2048]{1,0:T(8,128)(2,1)} async-done(((bf16[128,2048]{1,0:T(8,128)(2,1)}), bf16[1024,2048]{1,0:T(8,128)(2,1)}) %all-gather.21.cloned.1.call-update) | async-done | bytes 4194320 | tf_op jit(solution)/shard_map/all_gather | solution.py:51
  643.4 11.6 multiply_convert_fusion.2
  657.1 12.7 convolution_convert_fusion.1
  669.8 87.8 %reduce-scatter.13.cloned.1.call-done = bf16[128,2048]{1,0:T(8,128)(2,1)} async-done(((bf16[1024,2048]{1,0:T(8,128)(2,1)}), bf16[128,2048]{1,0:T(8,128)(2,1)}) %reduce-scatter.13.cloned.1.call-update) | async-done | bytes 524304 | tf_op jit(solution)/shard_map/reduce_scatter | solution.py:55
  759.4 3.3 fusion.33
  763.2 9.4 convolution_convert_fusion.4
  772.6 14.0 %convolution_convert_fusion = bf16[2048,2048]{1,0:T(8,128)(2,1)} fusion(bf16[1024,2048]{1,0:T(8,128)(2,1)} %all-gather.15.cloned.1.call-done, bf16[1024,1024]{1,0:T(8,128)(2,1)} %copy-done.24, bf16[1024,1024]{1,0:T(8,128)(2,1)} %copy-done.23), kind=kOutput, calls=%fused_computation.1 | convolution fusion | flops 8602517504 | bytes 16777216 | tf_op jit(solution)/shard_map/dot_general | solution.py:47
  786.9 22.9 %all-gather.23.cloned.1.call-done = bf16[1024,2048]{1,0:T(8,128)(2,1)} async-done(((bf16[128,2048]{1,0:T(8,128)(2,1)}), bf16[1024,2048]{1,0:T(8,128)(2,1)}) %all-gather.23.cloned.1.call-update) | async-done | bytes 4194320 | tf_op jit(solution)/shard_map/all_gather | solution.py:51
  809.8 4.6 convolution_convert_fusion.9
  818.3 3.4 multiply_reduce_fusion
  830.7 15.6 %psum.22 = f32[2,1024]{1,0:T(2,128)S(1)} all-reduce(f32[2,1024]{1,0:T(2,128)S(1)} %pad_maximum_fusion.11), channel_id=1, replica_groups=mesh['chip'=4,'core'=2,'ctx'=4] {'core','ctx'}, use_global_device_ids=true, to_apply=%region_15.16 | all-reduce | flops 2048 | bytes 16384 | tf_op jit(solution)/shard_map/psum | solution.py:174
  849.5 6.2 fusion.10
  855.9 7.7 convolution_convert_fusion.3
  863.7 4.3 broadcast_in_dim.35
  868.0 2.3 fusion.13
  870.4 5.7 all_to_all.77
  877.9 76.0 %reduce-scatter.21.cloned.1.call-done = bf16[512,2048]{1,0:T(8,128)(2,1)} async-done(((bf16[2048,2048]{1,0:T(8,128)(2,1)}), bf16[512,2048]{1,0:T(8,128)(2,1)}) %reduce-scatter.21.cloned.1.call-update) | async-done | bytes 2097168 | tf_op jit(solution)/shard_map/reduce_scatter | solution.py:55
  953.9 3.8 all-to-all-start.4
  957.6 43.1 %reduce-scatter.17.cloned.1.call-done = bf16[512,768]{0,1:T(8,128)(2,1)} async-done(((bf16[2048,768]{0,1:T(8,128)(2,1)}), bf16[512,768]{0,1:T(8,128)(2,1)}) %reduce-scatter.17.cloned.1.call-update) | async-done | bytes 786448 | tf_op jit(solution)/shard_map/reduce_scatter | solution.py:55
  1000.7 2.3 copy.133
  1003.0 4.6 all-to-all-start.3
  1007.6 64.0 %psum.23 = f32[4,2048]{1,0:T(4,128)} all-reduce(f32[4,2048]{1,0:T(4,128)S(1)} %pad_maximum_fusion.9), channel_id=1, replica_groups=mesh['chip'=4,'core'=2,'ctx'=4] {'chip','core','ctx'}, use_global_device_ids=true, to_apply=%region_25.26 | all-reduce | flops 8192 | bytes 65536 | tf_op jit(solution)/shard_map/psum | solution.py:196
  1071.6 2.5 convert_bitcast_fusion
  1074.1 6.6 reshape.191
  1080.7 7.3 fusion.67
  1089.6 2.2 copy.154
  1093.4 2.2 copy.155
  1095.6 2.6 reshape.193
  1100.8 5.9 reduce-scatter.15.cloned.1.call-done
  1106.6 2.2 add_bitcast_fusion
  1108.9 185.7 %reduce-scatter.19.cloned.1.call-done = bf16[64,2048]{1,0:T(8,128)(2,1)} async-done(((bf16[2048,2048]{1,0:T(8,128)(2,1)}), bf16[64,2048]{1,0:T(8,128)(2,1)}) %reduce-scatter.19.cloned.1.call-update) | async-done | bytes 262160 | tf_op jit(solution)/shard_map/reduce_scatter | solution.py:55
  (149 shorter events, 56.6 us)
Async XLA Ops:
  7.2 72.2 %all-gather.11.cloned.1.call-start = ((), (), s32[]{:S(2)}) async-start(), calls=%async_computation.14 | async-start | bytes 3932160 | tf_op jit(solution)/shard_map/all_gather | solution.py:51
  7.2 31.1 %copy-start.21 = (s32[1,128]{1,0:T(1,128)S(1)}, s32[1,128]{1,0:T(1,128)}, u32[]{:S(2)}) copy-start(s32[1,128]{1,0:T(1,128)} %param.10) | copy-start | bytes 1540
  7.2 45.0 %copy-start.20 = (f32[4,2048]{1,0:T(4,128)S(1)}, f32[4,2048]{1,0:T(4,128)}, u32[]{:S(2)}) copy-start(f32[4,2048]{1,0:T(4,128)} %param.16) | copy-start | bytes 98308
  36.8 91.3 %all-gather.25.cloned.1.call-start = ((), (), s32[]{:S(2)}) async-start(), calls=%async_computation.29 | async-start | bytes 4718592 | tf_op jit(solution)/shard_map/all_gather | solution.py:51
  37.5 170.0 %all-gather.13.cloned.1.call-start = ((), (), s32[]{:S(2)}) async-start(), calls=%async_computation.15 | async-start | bytes 8650752 | tf_op jit(solution)/shard_map/all_gather | solution.py:51
  38.3 261.6 %reduce-scatter.9.cloned.1.call-start = ((), (), s32[]{:S(2)}) async-start(), calls=%async_computation.16 | async-start | bytes 4718592 | tf_op jit(solution)/shard_map/reduce_scatter | solution.py:55
  168.0 2.8 copy-start.4
  168.0 2.8 copy-start.5
  168.0 2.8 copy-start.13
  168.0 2.8 copy-start.14
  212.2 177.4 %all-gather.17.cloned.1.call-start = ((), (), s32[]{:S(2)}) async-start(), calls=%async_computation.18 | async-start | bytes 10485760 | tf_op jit(solution)/shard_map/all_gather | solution.py:51
  228.8 210.0 %all-gather.15.cloned.1.call-start = ((), (), s32[]{:S(2)}) async-start(), calls=%async_computation.17 | async-start | bytes 4718592 | tf_op jit(solution)/shard_map/all_gather | solution.py:51
  303.4 189.2 %all-gather.19.cloned.1.call-start = ((), (), s32[]{:S(2)}) async-start(), calls=%async_computation.19 | async-start | bytes 5242880 | tf_op jit(solution)/shard_map/all_gather | solution.py:51
  314.8 276.3 %reduce-scatter.11.cloned.1.call-start = ((), (), s32[]{:S(2)}) async-start(), calls=%async_computation.20 | async-start | bytes 4718592 | tf_op jit(solution)/shard_map/reduce_scatter | solution.py:55
  451.3 3.2 copy-start.7
  502.0 141.5 %all-gather.21.cloned.1.call-start = ((), (), s32[]{:S(2)}) async-start(), calls=%async_computation.21 | async-start | bytes 4718592 | tf_op jit(solution)/shard_map/all_gather | solution.py:51
  596.4 161.2 %reduce-scatter.13.cloned.1.call-start = ((), (), s32[]{:S(2)}) async-start(), calls=%async_computation.22 | async-start | bytes 4718592 | tf_op jit(solution)/shard_map/reduce_scatter | solution.py:55
  655.1 1.3 copy-start.23
  655.1 2.0 copy-start.24
  669.7 140.0 %all-gather.23.cloned.1.call-start = ((), (), s32[]{:S(2)}) async-start(), calls=%async_computation.23 | async-start | bytes 4718592 | tf_op jit(solution)/shard_map/all_gather | solution.py:51
  762.7 107.6 %reduce-scatter.23.cloned.1.call-start = ((), (), s32[]{:S(2)}) async-start(), calls=%async_computation.28 | async-start | bytes 5242880 | tf_op jit(solution)/shard_map/reduce_scatter | solution.py:55
  772.6 181.3 %reduce-scatter.21.cloned.1.call-start = ((), (), s32[]{:S(2)}) async-start(), calls=%async_computation.27 | async-start | bytes 10485760 | tf_op jit(solution)/shard_map/reduce_scatter | solution.py:55
  786.7 214.1 %reduce-scatter.17.cloned.1.call-start = ((), (), s32[]{:S(2)}) async-start(), calls=%async_computation.25 | async-start | bytes 3932160 | tf_op jit(solution)/shard_map/reduce_scatter | solution.py:55
  818.3 3.8 copy-start.9
  822.1 1.2 copy-start.11
  822.1 2.0 copy-start.10
  824.1 1.0 copy-start.12
  825.6 2.1 copy-start.17
  826.7 3.3 copy-start.2
  827.7 2.3 copy-start.3
  846.3 3.2 copy-start.18
  846.3 3.1 copy-start.22
  848.5 0.8 copy-start.15
  848.5 1.0 copy-start.16
  849.5 6.5 copy-start.19
  855.7 251.0 %reduce-scatter.15.cloned.1.call-start = ((), (), s32[]{:S(2)}) async-start(), calls=%async_computation.24 | async-start | bytes 4718592 | tf_op jit(solution)/shard_map/reduce_scatter | solution.py:55
  863.7 4.4 copy-start.6
  863.7 430.9 %reduce-scatter.19.cloned.1.call-start = ((), (), s32[]{:S(2)}) async-start(), calls=%async_computation.26 | async-start | bytes 8650752 | tf_op jit(solution)/shard_map/reduce_scatter | solution.py:55
  863.7 4.3 copy-start.1
  953.9 49.1 %all-to-all-start.4 = ((bf16[2,256,2048]{2,1,0:T(8,128)(2,1)}), bf16[2,256,2048]{2,1,0:T(8,128)(2,1)S(1)}, u32[]{:S(2)}, u32[]{:S(2)}) async-start(bf16[2,256,2048]{2,1,0:T(8,128)(2,1)} %bitcast.167), calls=%async_computation.11 | async-start | bytes 4194304 | tf_op jit(solution)/shard_map/all_to_all | solution.py:151
  1003.0 92.6 %all-to-all-start.3 = ((bf16[8,64,768]{2,1,0:T(8,128)(2,1)}), bf16[8,64,768]{2,1,0:T(8,128)(2,1)}, u32[]{:S(2)}, u32[]{:S(2)}) async-start(bf16[8,64,768]{2,1,0:T(8,128)(2,1)} %bitcast.33), calls=%async_computation.8 | async-start | bytes 1572864 | tf_op jit(solution)/shard_map/all_to_all | solution.py:186
  1095.6 11.0 copy-start
  1095.6 11.0 copy-start.8
Sparse Core Ops, SparseCore 0:
  36.9 42.3 all-gather.10
  80.9 47.1 all-gather.24
  131.0 76.4 all-gather.12
  212.3 87.5 reduce-scatter.8
  302.2 87.3 all-gather.16
  391.6 47.1 all-gather.14
  441.2 51.4 all-gather.18
  502.1 88.9 reduce-scatter.10
  596.5 46.9 all-gather.20
  669.9 87.6 reduce-scatter.12
  762.9 46.8 all-gather.22
  812.6 51.4 reduce-scatter.22
  867.4 86.4 reduce-scatter.20
  956.7 43.9 reduce-scatter.16
  1002.9 103.7 reduce-scatter.14
  1108.8 185.7 reduce-scatter.18
where the time goes:
time: 1310 us; the launch traced here: 1300 us
  waiting for transfers between devices  885 us (68%)
  blocking collectives  153 us (12%)
  matrix products  116 us (9%)
  local copies, waits for them, and re-layouts  83.7 us (6%)
  other arithmetic  39.8 us (3%)
  between operations  14.9 us (1%)
    reduce_scatter x8, waiting for transfers between devices, scatter_sum(): return lax.psum_scatter(values, axes, scatter_dimension=0, tiled=True)  559 us
    all_gather x8, waiting for transfers between devices, gather(): return lax.all_gather(values, axes, axis=0, tiled=True)  325 us
    psum x1, blocking collectives, per_device(): lax.psum(jnp.concatenate([wide, gain_attn[None], gain_feed[None]]), ALL)  64 us
    dot_general x4, matrix products, dot(): return jnp.dot(left, right, preferred_element_type=F32)  34.9 us
    dot_general x4, matrix products, dot_rows(): lax.dot_general(left, right, (((1,), (1,)), ((), ())), preferred_element_...  34.2 us
    dot_general x4, matrix products, dot_first(): lax.dot_general(left, right, (((0,), (0,)), ((), ())), preferred_element_...  31.8 us
    all_to_all x1, blocking collectives, per_device(): qkv_cut = lax.all_to_all(qkv_cut, GROUP, 0, 0, tiled=True)  26.9 us
  transfers between devices with their start and end apart: 18, of which 15 were waited for; matrix products, arithmetic and copies ran while one was open for 14% of the time, Pallas kernels for 0%

commit v1 on v0

--- a/solution.py
+++ b/solution.py
@@ -193,7 +193,9 @@
     grad_out = scatter_sum(out_part, ALL).astype(F32)
     wide = jnp.zeros((2, width), F32)
     wide = lax.dynamic_update_slice(wide, jnp.stack([gain_query, gain_key]), (0, member * part))
-    grad_gains = lax.psum(jnp.concatenate([wide, gain_attn[None], gain_feed[None]]), ALL)
+    grad_gains = jnp.concatenate([wide, gain_attn[None], gain_feed[None]])
+    for mesh_axis in ("chip", ("core", "ctx")):
+        grad_gains = lax.psum(grad_gains, mesh_axis)
     return (
         output[None],
         input_grad[None],

time: 1310 us -> 1320 us (level)
  waiting for transfers between devices: 885 us -> 934 us
  blocking collectives: 153 us -> 120 us
    psum x1, blocking collectives: 64 us -> 16.8 us  [per_device(): grad_gains = lax.psum(grad_gains, mesh_axis)]
    reduce_scatter x8, waiting for transfers between devices: 559 us -> 578 us  [scatter_sum(): return lax.psum_scatter(values, axes, scatter_dimension=0, tiled=True)]
    all_to_all x1, waiting for transfers between devices: 0.01 us -> 15.9 us  [per_device(): grad_qkv = lax.all_to_all(grad_qkv, GROUP, 0, 0, tiled=True)]
    all_gather x8, waiting for transfers between devices: 325 us -> 339 us  [gather(): return lax.all_gather(values, axes, axis=0, tiled=True)]
    unnamed x62 -> x68, local copies, waits for them, and re-layouts: 25.5 us -> 26.9 us
  transfers between devices with their start and end apart: 18 -> 18, of which waited for: 15 -> 16; matrix products, arithmetic and copies ran while one was open for 14% -> 14% of each run, Pallas kernels for 0% -> 0%
where the time goes in v1:
time: 1320 us
  waiting for transfers between devices  934 us (71%)
  blocking collectives  120 us (9%)
  matrix products  116 us (9%)
  local copies, waits for them, and re-layouts  84.9 us (6%)
  other arithmetic  39.8 us (3%)
  between operations  14.8 us (1%)
    reduce_scatter x8, waiting for transfers between devices, scatter_sum(): return lax.psum_scatter(values, axes, scatter_dimension=0, tiled=True)  578 us
    all_gather x8, waiting for transfers between devices, gather(): return lax.all_gather(values, axes, axis=0, tiled=True)  339 us
    dot_general x4, matrix products, dot(): return jnp.dot(left, right, preferred_element_type=F32)  34.9 us
    dot_general x4, matrix products, dot_rows(): lax.dot_general(left, right, (((1,), (1,)), ((), ())), preferred_element_...  33.7 us
    dot_general x4, matrix products, dot_first(): lax.dot_general(left, right, (((0,), (0,)), ((), ())), preferred_element_...  31.6 us
    psum x1, blocking collectives, per_device(): means = lax.psum(sums, GROUP) / width  28 us
    unnamed x68, local copies, waits for them, and re-layouts  26.9 us
    all_to_all x1, blocking collectives, per_device(): qkv_cut = lax.all_to_all(qkv_cut, GROUP, 0, 0, tiled=True)  26.9 us
  transfers between devices with their start and end apart: 18, of which 16 were waited for; matrix products, arithmetic and copies ran while one was open for 14% of the time, Pallas kernels for 0%

profile of v1, /device:TPU:0, one launch (start us, length us, event | category | flops | bytes accessed | tf_op | source)
XLA Modules:
  0.0 1318.8 jit_solution(9574531186830737172)
XLA Ops:
  9.9 26.9 %all_to_all.74 = bf16[8,64,768]{2,1,0:T(8,128)(2,1)} all-to-all(bf16[8,64,768]{2,1,0:T(8,128)(2,1)S(1)} %reshape.177), channel_id=1, replica_groups=mesh['chip'=4,'core'=2,'ctx'=4] {'core','ctx'}, dimensions={0} | all-to-all | bytes 1572864 | tf_op jit(solution)/shard_map/all_to_all | solution.py:83
  38.3 12.7 all-gather.1
  55.4 23.9 %all-gather.11.cloned.1.call-done = bf16[2048,768]{1,0:T(8,128)(2,1)} async-done(((bf16[512,768]{1,0:T(8,128)(2,1)}), bf16[2048,768]{1,0:T(8,128)(2,1)}) %all-gather.11.cloned.1.call-update) | async-done | bytes 3145744 | tf_op jit(solution)/shard_map/all_gather | solution.py:51
  79.3 48.8 %all-gather.25.cloned.1.call-done = bf16[1,1024,2048]{2,1,0:T(8,128)(2,1)} async-done(((bf16[1,128,2048]{2,1,0:T(8,128)(2,1)}), bf16[1,1024,2048]{2,1,0:T(8,128)(2,1)}) %all-gather.25.cloned.1.call-update) | async-done | bytes 4194320 | tf_op jit(solution)/shard_map/all_gather | solution.py:51
  128.1 6.2 fusion.3
  135.4 15.6 %psum.28 = f32[2,1024]{1,0:T(2,128)S(1)} all-reduce(f32[2,1024]{1,0:T(2,128)S(1)} %pad_maximum_fusion.10), channel_id=1, replica_groups=mesh['chip'=4,'core'=2,'ctx'=4] {'core','ctx'}, use_global_device_ids=true, to_apply=%region_2.0 | all-reduce | flops 2048 | bytes 16384 | tf_op jit(solution)/shard_map/psum | solution.py:100
  152.6 3.1 reshape.181
  155.7 2.6 copy.109
  158.3 3.1 reshape.180
  161.4 2.4 copy.106
  163.8 2.2 reshape.179
  172.5 5.9 fusion.73
  178.4 4.1 fusion.25
  184.5 23.1 %all-gather.13.cloned.1.call-done = bf16[2048,2048]{1,0:T(8,128)(2,1)} async-done(((bf16[64,2048]{1,0:T(8,128)(2,1)}), bf16[2048,2048]{1,0:T(8,128)(2,1)}) %all-gather.13.cloned.1.call-update) | async-done | bytes 8388624 | tf_op jit(solution)/shard_map/all_gather | solution.py:51
  207.6 4.6 convolution_convert_fusion.2
  212.3 2.3 copy.117
  214.5 2.3 copy.118
  218.6 6.3 all_to_all.75
  224.9 3.9 copy.119
  228.9 71.0 %reduce-scatter.9.cloned.1.call-done = bf16[128,2048]{1,0:T(8,128)(2,1)} async-done(((bf16[1024,2048]{1,0:T(8,128)(2,1)}), bf16[128,2048]{1,0:T(8,128)(2,1)}) %reduce-scatter.9.cloned.1.call-update) | async-done | bytes 524304 | tf_op jit(solution)/shard_map/reduce_scatter | solution.py:55
  301.2 2.3 fusion.49
  303.5 2.3 copy.120
  305.8 6.6 all_to_all.76
  312.4 2.4 copy.121
  315.1 74.5 %all-gather.17.cloned.1.call-done = bf16[2048,2048]{1,0:T(8,128)(2,1)} async-done(((bf16[512,2048]{1,0:T(8,128)(2,1)}), bf16[2048,2048]{1,0:T(8,128)(2,1)}) %all-gather.17.cloned.1.call-update) | async-done | bytes 8388624 | tf_op jit(solution)/shard_map/all_gather | solution.py:51
  389.6 49.2 %all-gather.15.cloned.1.call-done = bf16[1024,2048]{1,0:T(8,128)(2,1)} async-done(((bf16[128,2048]{1,0:T(8,128)(2,1)}), bf16[1024,2048]{1,0:T(8,128)(2,1)}) %all-gather.15.cloned.1.call-update) | async-done | bytes 4194320 | tf_op jit(solution)/shard_map/all_gather | solution.py:51
  438.8 12.5 fusion.74
  451.3 3.3 copy-done.7
  454.5 2.7 multiply_convert_fusion.3
  457.3 35.4 %all-gather.19.cloned.1.call-done = bf16[2048,1024]{1,0:T(8,128)(2,1)} async-done(((bf16[512,1024]{1,0:T(8,128)(2,1)}), bf16[2048,1024]{1,0:T(8,128)(2,1)}) %all-gather.19.cloned.1.call-update) | async-done | bytes 4194320 | tf_op jit(solution)/shard_map/all_gather | solution.py:51
  492.7 9.3 convolution_convert_fusion.5
  502.0 89.1 %reduce-scatter.11.cloned.1.call-done = bf16[128,2048]{1,0:T(8,128)(2,1)} async-done(((bf16[1024,2048]{1,0:T(8,128)(2,1)}), bf16[128,2048]{1,0:T(8,128)(2,1)}) %reduce-scatter.11.cloned.1.call-update) | async-done | bytes 524304 | tf_op jit(solution)/shard_map/reduce_scatter | solution.py:55
  594.0 2.4 fusion.28
  596.7 46.8 %all-gather.21.cloned.1.call-done = bf16[1024,2048]{1,0:T(8,128)(2,1)} async-done(((bf16[128,2048]{1,0:T(8,128)(2,1)}), bf16[1024,2048]{1,0:T(8,128)(2,1)}) %all-gather.21.cloned.1.call-update) | async-done | bytes 4194320 | tf_op jit(solution)/shard_map/all_gather | solution.py:51
  643.5 11.6 multiply_convert_fusion.2
  657.1 12.6 convolution_convert_fusion.1
  669.8 87.8 %reduce-scatter.13.cloned.1.call-done = bf16[128,2048]{1,0:T(8,128)(2,1)} async-done(((bf16[1024,2048]{1,0:T(8,128)(2,1)}), bf16[128,2048]{1,0:T(8,128)(2,1)}) %reduce-scatter.13.cloned.1.call-update) | async-done | bytes 524304 | tf_op jit(solution)/shard_map/reduce_scatter | solution.py:55
  759.4 3.3 fusion.33
  762.8 9.4 convolution_convert_fusion.4
  772.6 37.1 %all-gather.23.cloned.1.call-done = bf16[1024,2048]{1,0:T(8,128)(2,1)} async-done(((bf16[128,2048]{1,0:T(8,128)(2,1)}), bf16[1024,2048]{1,0:T(8,128)(2,1)}) %all-gather.23.cloned.1.call-update) | async-done | bytes 4194320 | tf_op jit(solution)/shard_map/all_gather | solution.py:51
  809.8 4.6 convolution_convert_fusion.9
  818.3 3.4 multiply_reduce_fusion
  830.7 16.8 %psum.30 = f32[4,2048]{1,0:T(4,128)S(1)} all-reduce(f32[4,2048]{1,0:T(4,128)S(1)} %pad_maximum_fusion.9), channel_id=1, replica_groups=mesh['chip'=4,'core'=2,'ctx'=4] {'chip'}, use_global_device_ids=true, to_apply=%region_25.26 | all-reduce | flops 8192 | bytes 65536 | tf_op jit(solution)/shard_map/psum | solution.py:198
  847.5 28.0 %all-reduce = (f32[2,1024]{1,0:T(2,128)S(1)}, f32[4,2048]{1,0:T(4,128)}) all-reduce(f32[2,1024]{1,0:T(2,128)S(1)} %pad_maximum_fusion.11, f32[4,2048]{1,0:T(4,128)S(1)} %psum.30), channel_id=1, replica_groups=mesh['chip'=4,'core'=2,'ctx'=4] {'core','ctx'}, use_global_device_ids=true, to_apply=%region_15.16 | all-reduce | flops 10240 | bytes 81920 | tf_op jit(solution)/shard_map/psum | solution.py:174
  878.7 6.2 fusion.10
  885.0 13.6 %convolution_convert_fusion = bf16[2048,2048]{1,0:T(8,128)(2,1)} fusion(bf16[1024,2048]{1,0:T(8,128)(2,1)} %all-gather.15.cloned.1.call-done, bf16[1024,1024]{1,0:T(8,128)(2,1)} %copy-done.27, bf16[1024,1024]{1,0:T(8,128)(2,1)S(1)} %copy-done.26), kind=kOutput, calls=%fused_computation.1 | convolution fusion | flops 8602517504 | bytes 16777216 | tf_op jit(solution)/shard_map/dot_general | solution.py:47
  900.1 7.2 convolution_convert_fusion.3
  907.4 4.3 broadcast_in_dim.35
  911.7 2.4 fusion.13
  914.1 3.6 all-to-all-start.5
  917.7 9.2 reduce-scatter.17.cloned.1.call-done
  926.9 2.3 copy.133
  929.2 87.4 %reduce-scatter.21.cloned.1.call-done = bf16[512,2048]{1,0:T(8,128)(2,1)} async-done(((bf16[2048,2048]{1,0:T(8,128)(2,1)}), bf16[512,2048]{1,0:T(8,128)(2,1)}) %reduce-scatter.21.cloned.1.call-update) | async-done | bytes 2097168 | tf_op jit(solution)/shard_map/reduce_scatter | solution.py:55
  1016.5 6.6 all_to_all.77
  1023.1 4.9 all-to-all-start.3
  1029.7 2.5 convert_bitcast_fusion
  1032.2 6.6 reshape.191
  1038.8 7.2 fusion.67
  1047.6 2.2 copy.154
  1053.6 15.9 %all-to-all-done.3 = bf16[8,64,768]{2,1,0:T(8,128)(2,1)} async-done(((bf16[8,64,768]{2,1,0:T(8,128)(2,1)}), bf16[8,64,768]{2,1,0:T(8,128)(2,1)}, u32[]{:S(2)}, u32[]{:S(2)}) %all-to-all-start.3) | async-done | bytes 786464 | tf_op jit(solution)/shard_map/all_to_all | solution.py:186
  1069.6 2.5 reshape.193
  1074.6 46.3 %reduce-scatter.15.cloned.1.call-done = bf16[128,2048]{1,0:T(8,128)(2,1)} async-done(((bf16[1024,2048]{1,0:T(8,128)(2,1)}), bf16[128,2048]{1,0:T(8,128)(2,1)}) %reduce-scatter.15.cloned.1.call-update) | async-done | bytes 524304 | tf_op jit(solution)/shard_map/reduce_scatter | solution.py:55
  1120.9 2.2 add_bitcast_fusion
  1123.1 187.2 %reduce-scatter.19.cloned.1.call-done = bf16[64,2048]{1,0:T(8,128)(2,1)} async-done(((bf16[2048,2048]{1,0:T(8,128)(2,1)}), bf16[64,2048]{1,0:T(8,128)(2,1)}) %reduce-scatter.19.cloned.1.call-update) | async-done | bytes 262160 | tf_op jit(solution)/shard_map/reduce_scatter | solution.py:55
  (155 shorter events, 59.7 us)
Async XLA Ops:
  7.2 72.2 %all-gather.11.cloned.1.call-start = ((), (), s32[]{:S(2)}) async-start(), calls=%async_computation.14 | async-start | bytes 3932160 | tf_op jit(solution)/shard_map/all_gather | solution.py:51
  7.2 31.1 %copy-start.23 = (s32[1,128]{1,0:T(1,128)S(1)}, s32[1,128]{1,0:T(1,128)}, u32[]{:S(2)}) copy-start(s32[1,128]{1,0:T(1,128)} %param.10) | copy-start | bytes 1540
  7.2 45.0 %copy-start.22 = (f32[4,2048]{1,0:T(4,128)S(1)}, f32[4,2048]{1,0:T(4,128)}, u32[]{:S(2)}) copy-start(f32[4,2048]{1,0:T(4,128)} %param.16) | copy-start | bytes 98308
  36.8 91.3 %all-gather.25.cloned.1.call-start = ((), (), s32[]{:S(2)}) async-start(), calls=%async_computation.29 | async-start | bytes 4718592 | tf_op jit(solution)/shard_map/all_gather | solution.py:51
  37.5 170.0 %all-gather.13.cloned.1.call-start = ((), (), s32[]{:S(2)}) async-start(), calls=%async_computation.15 | async-start | bytes 8650752 | tf_op jit(solution)/shard_map/all_gather | solution.py:51
  38.3 261.7 %reduce-scatter.9.cloned.1.call-start = ((), (), s32[]{:S(2)}) async-start(), calls=%async_computation.16 | async-start | bytes 4718592 | tf_op jit(solution)/shard_map/reduce_scatter | solution.py:55
  168.0 2.8 copy-start.4
  168.0 2.8 copy-start.5
  168.0 2.8 copy-start.13
  168.0 2.8 copy-start.14
  212.2 177.4 %all-gather.17.cloned.1.call-start = ((), (), s32[]{:S(2)}) async-start(), calls=%async_computation.18 | async-start | bytes 10485760 | tf_op jit(solution)/shard_map/all_gather | solution.py:51
  228.9 209.9 %all-gather.15.cloned.1.call-start = ((), (), s32[]{:S(2)}) async-start(), calls=%async_computation.17 | async-start | bytes 4718592 | tf_op jit(solution)/shard_map/all_gather | solution.py:51
  303.4 189.2 %all-gather.19.cloned.1.call-start = ((), (), s32[]{:S(2)}) async-start(), calls=%async_computation.19 | async-start | bytes 5242880 | tf_op jit(solution)/shard_map/all_gather | solution.py:51
  314.9 276.3 %reduce-scatter.11.cloned.1.call-start = ((), (), s32[]{:S(2)}) async-start(), calls=%async_computation.20 | async-start | bytes 4718592 | tf_op jit(solution)/shard_map/reduce_scatter | solution.py:55
  451.3 3.3 copy-start.7
  502.0 141.5 %all-gather.21.cloned.1.call-start = ((), (), s32[]{:S(2)}) async-start(), calls=%async_computation.21 | async-start | bytes 4718592 | tf_op jit(solution)/shard_map/all_gather | solution.py:51
  596.4 161.2 %reduce-scatter.13.cloned.1.call-start = ((), (), s32[]{:S(2)}) async-start(), calls=%async_computation.22 | async-start | bytes 4718592 | tf_op jit(solution)/shard_map/reduce_scatter | solution.py:55
  655.1 1.3 copy-start.25
  655.1 2.0 copy-start.27
  669.7 140.0 %all-gather.23.cloned.1.call-start = ((), (), s32[]{:S(2)}) async-start(), calls=%async_computation.23 | async-start | bytes 4718592 | tf_op jit(solution)/shard_map/all_gather | solution.py:51
  762.7 151.4 %reduce-scatter.23.cloned.1.call-start = ((), (), s32[]{:S(2)}) async-start(), calls=%async_computation.28 | async-start | bytes 5242880 | tf_op jit(solution)/shard_map/reduce_scatter | solution.py:55
  772.2 154.7 %reduce-scatter.17.cloned.1.call-start = ((), (), s32[]{:S(2)}) async-start(), calls=%async_computation.25 | async-start | bytes 3932160 | tf_op jit(solution)/shard_map/reduce_scatter | solution.py:55
  818.3 3.8 copy-start.9
  822.1 1.2 copy-start.11
  822.1 2.0 copy-start.10
  824.1 1.0 copy-start.12
  825.6 2.1 copy-start.21
  826.7 3.3 copy-start.2
  827.7 2.3 copy-start.3
  875.5 3.1 copy-start.19
  875.5 3.1 copy-start.24
  877.7 0.8 copy-start.15
  877.7 1.0 copy-start.17
  878.7 6.3 copy-start.26
  884.9 131.6 %reduce-scatter.21.cloned.1.call-start = ((), (), s32[]{:S(2)}) async-start(), calls=%async_computation.27 | async-start | bytes 10485760 | tf_op jit(solution)/shard_map/reduce_scatter | solution.py:55
  898.6 1.1 copy-start.16
  898.6 1.3 copy-start.18
  898.6 1.5 copy-start.20
  898.6 222.2 %reduce-scatter.15.cloned.1.call-start = ((), (), s32[]{:S(2)}) async-start(), calls=%async_computation.24 | async-start | bytes 4718592 | tf_op jit(solution)/shard_map/reduce_scatter | solution.py:55
  907.3 4.4 copy-start.6
  907.3 403.0 %reduce-scatter.19.cloned.1.call-start = ((), (), s32[]{:S(2)}) async-start(), calls=%async_computation.26 | async-start | bytes 8650752 | tf_op jit(solution)/shard_map/reduce_scatter | solution.py:55
  907.4 4.3 copy-start.1
  914.1 15.0 %all-to-all-start.5 = ((bf16[2,256,1024]{2,1,0:T(8,128)(2,1)}), bf16[2,256,1024]{2,1,0:T(8,128)(2,1)S(1)}, u32[]{:S(2)}, u32[]{:S(2)}) async-start(bf16[2,256,1024]{2,1,0:T(8,128)(2,1)} %bitcast.174), calls=%async_computation.13 | async-start | bytes 2097152 | tf_op jit(solution)/shard_map/all_to_all | solution.py:156
  1023.1 46.4 %all-to-all-start.3 = ((bf16[8,64,768]{2,1,0:T(8,128)(2,1)}), bf16[8,64,768]{2,1,0:T(8,128)(2,1)}, u32[]{:S(2)}, u32[]{:S(2)}) async-start(bf16[8,64,768]{2,1,0:T(8,128)(2,1)} %bitcast.167), calls=%async_computation.8 | async-start | bytes 1572864 | tf_op jit(solution)/shard_map/all_to_all | solution.py:186
  1053.6 67.2 %copy-start = (bf16[1,128,2048]{2,1,0:T(8,128)(2,1)S(1)}, bf16[1,128,2048]{2,1,0:T(8,128)(2,1)}, u32[]{:S(2)}) copy-start(bf16[1,128,2048]{2,1,0:T(8,128)(2,1)} %param.17) | copy-start | bytes 1572868
  1053.6 67.2 %copy-start.8 = (bf16[128,2048]{1,0:T(8,128)(2,1)S(1)}, bf16[128,2048]{1,0:T(8,128)(2,1)}, u32[]{:S(2)}) copy-start(bf16[128,2048]{1,0:T(8,128)(2,1)} %reduce-scatter.13.cloned.1.call-done) | copy-start | bytes 1572868
Sparse Core Ops, SparseCore 0:
  36.9 42.3 all-gather.10
  80.9 47.1 all-gather.24
  131.0 76.4 all-gather.12
  212.3 87.5 reduce-scatter.8
  302.2 87.3 all-gather.16
  391.6 47.1 all-gather.14
  441.2 51.4 all-gather.18
  502.1 88.9 reduce-scatter.10
  596.5 46.8 all-gather.20
  669.9 87.6 reduce-scatter.12
  762.9 46.8 all-gather.22
  812.6 52.2 reduce-scatter.22
  885.0 41.7 reduce-scatter.16
  930.1 86.3 reduce-scatter.20
  1018.6 102.1 reduce-scatter.14
  1123.0 187.2 reduce-scatter.18
